TPU v7x, 32 devices: a whole 2x2x4 slice. The times are simulated.
32 devices in a mesh: sec: 4 (over x, core), lat: 2 (over y), col: 4 (over z).
Axes of the slice: x: 2, y: 2, z: 4, core: 2. Of those that a mesh axis runs over, the one named last changes fastest.
Arguments:
- state: float32 [1, 4, 28, 192, 384], P(None, 'sec', None, 'lat', 'col'), may hold values from -6 to 6
- forcing: float32 [1, 4, 28, 192, 384], P(None, 'sec', None, 'lat', 'col'), may hold values from -4 to 4
- crm_moisture: bfloat16 [1, 32, 28, 8, 4, 2304], P(None, None, None, ('sec', 'lat'), 'col'), may hold values from -6 to 6
- cloud_order: int32 [4, 2, 9216], P('col', 'lat'), may hold values from 0 to 9215, each once within a row
- wave_table: int32 [128], replicated, may hold values from 0 to 127, each once
Outputs:
- state_out: float32 [1, 4, 28, 192, 384], P(None, 'sec', None, 'lat', 'col')
- spectral: float32 [4, 1, 28, 128, 2, 128], P('sec', None, 'col', 'lat')
Inputs may be any that keep to these rules, and one draw needn't show every extreme that they name: `cloud_order`: every row lists each of the 9216 columns of a band block once. `wave_table`: each wavenumber stands in exactly one slot.
All inputs are finite; a program needn't handle non-finite values.
Results may differ from a plain program's by a relative error of at most 0.0003.
Values sent between devices are 32-bit elements; how exact they have to be, the bound alone decides.
A program may use at most 128 MiB of HBM per device.

v0:
```python
import math

import jax
import jax.numpy as jnp
from jax import lax
from jax.experimental import pallas as pl
from jax.experimental.pallas import tpu as pltpu
from jax.sharding import PartitionSpec as P

NLON = 384
NLAT = 192
MMAX = 128
NSUB = 4
LANES = 128
ROWS = 8

COURANT_SCALE = 0.4
CONDENSE = 0.5


def permute_kernel(x_ref, order_ref, out_ref, parts, held):
    levels = x_ref.shape[-2]
    rows = held.shape[0]
    cols = order_ref.shape[1]
    tiles = cols // LANES
    gathered = held.shape[1] // LANES
    multiplied = tiles - gathered
    halves = 2 if tiles % 2 == 0 else 1
    width = halves * LANES
    fill = jnp.zeros((rows - levels, LANES), jnp.float32)
    groups = range(rows // ROWS)

    for s in range(tiles):
        if x_ref.ndim == 2:
            block = x_ref[:, s * LANES : (s + 1) * LANES]
        else:
            per = x_ref.shape[2] // LANES
            block = x_ref[s // per, :, s % per * LANES : (s % per + 1) * LANES]
        if rows > levels:
            block = jnp.concatenate([block, fill], axis=0)
        if s < multiplied:
            coarse = block.astype(jnp.bfloat16)
            parts[s * rows : (s + 1) * rows, :LANES] = coarse
            parts[s * rows : (s + 1) * rows, LANES:] = (
                block - coarse.astype(jnp.float32)
            ).astype(jnp.bfloat16)
        else:
            held[:, (s - multiplied) * LANES : (s - multiplied + 1) * LANES] = block
    wanted = lax.broadcasted_iota(jnp.int32, (2 * LANES, width), 0) & (LANES - 1)

    def one(t, carry):
        order = order_ref[:, pl.ds(pl.multiple_of(t * width, width), width)]
        lane = order & (LANES - 1)
        chosen = jnp.where(wanted == lane, 1.0, 0.0).astype(jnp.bfloat16)
        moved = jnp.dot(parts[...], chosen, preferred_element_type=jnp.float32)
        for h in range(halves):
            mine = slice(h * LANES, (h + 1) * LANES)
            source = jnp.broadcast_to(order[:, mine] >> 7, (ROWS, LANES))
            lanes = jnp.broadcast_to(lane[:, mine], (ROWS, LANES))
            total = [jnp.zeros((ROWS, LANES), jnp.float32) for _ in groups]
            for s in range(gathered):
                hit = source == multiplied + s
                for r in groups:
                    block = held[r * ROWS : (r + 1) * ROWS, s * LANES : (s + 1) * LANES]
                    total[r] = jnp.where(hit, jnp.take_along_axis(block, lanes, axis=1), total[r])
            for s in range(multiplied):
                hit = source == s
                for r in groups:
                    begin = s * rows + r * ROWS
                    total[r] = jnp.where(hit, moved[begin : begin + ROWS, mine], total[r])
            tile = t * halves + h
            for r in groups:
                end = min((r + 1) * ROWS, levels)
                value = total[r][: end - r * ROWS]
                if out_ref.ndim == 2:
                    at = pl.ds(pl.multiple_of(tile * LANES, LANES), LANES)
                    out_ref[r * ROWS : end, at] = value
                else:
                    per = out_ref.shape[2] // LANES
                    at = pl.ds(pl.multiple_of(tile % per * LANES, LANES), LANES)
                    out_ref[tile // per, r * ROWS : end, at] = value
        return carry

    lax.fori_loop(0, tiles // halves, one, 0)


def permute(values, order, shape):
    levels, tiles = values.shape[-2], order.shape[1] // LANES
    rows = -(-levels // ROWS) * ROWS
    gathered = tiles * 3 // 8
    return pl.pallas_call(
        permute_kernel,
        out_shape=jax.ShapeDtypeStruct(shape, jnp.float32),
        in_specs=[pl.BlockSpec(memory_space=pltpu.VMEM)] * 2,
        out_specs=pl.BlockSpec(memory_space=pltpu.VMEM),
        scratch_shapes=[
            pltpu.VMEM(((tiles - gathered) * rows, 2 * LANES), jnp.bfloat16),
            pltpu.VMEM((rows, gathered * LANES), jnp.float32),
        ],
        name="permute",
    )(values, order)


def cloud_kernel(wind_ref, gap_ref, push_ref, anomaly_ref, rain_ref):
    count, levels, width = anomaly_ref.shape
    scale = CONDENSE / count

    for c0 in range(0, width, LANES):
        c1 = min(c0 + LANES, width)
        for base in range(0, levels, 2 * ROWS):
            top = min(base + 2 * ROWS, levels)
            for r0 in range(base, top, ROWS):
                r1 = min(r0 + ROWS, top)
                courant = COURANT_SCALE * jnp.tanh(wind_ref[r0:r1, c0:c1])
                mixing = 0.2 + 0.5 * jnp.abs(courant)
                ahead = mixing - 0.5 * courant
                back = mixing + 0.5 * courant
                keep = 1.0 - 2.0 * mixing
                push = push_ref[r0:r1, c0:c1]
                start = gap_ref[r0:r1, c0:c1]
                gap = [
                    start
                    + anomaly_ref[n, base:top, c0:c1].astype(jnp.float32)[r0 - base : r1 - base]
                    for n in range(count)
                ]
                rain = [jnp.zeros_like(start) for _ in range(2)]
                for substep in range(NSUB):
                    fresh = []
                    for n in range(count):
                        wet = jnp.maximum(gap[n], 0.0)
                        rain[n % 2] = rain[n % 2] + wet
                        if substep < NSUB - 1:
                            fresh.append(
                                (ahead * gap[(n + 1) % count] + back * gap[n - 1])
                                + (keep * gap[n] + (push - wet))
                            )
                    gap = fresh
                found = scale * (rain[0] + rain[1])
                for copy in range(rain_ref.shape[0]):
                    rain_ref[copy, r0:r1, c0:c1] = found


def cloud_model(arrived, anomaly, sections):
    count, levels, _ = anomaly.shape
    blocks, _, span = arrived.shape
    bands = blocks // sections
    block = LANES if span % LANES == 0 else span
    steps = span // block
    if block < LANES:
        anomaly = anomaly.reshape(count, levels, bands, span).transpose(2, 0, 1, 3)
        moist = pl.BlockSpec((None, count, levels, span), lambda i: (i, 0, 0, 0))
    else:
        moist = pl.BlockSpec((count, levels, block), lambda i: (0, 0, i))

    def of(field):
        return pl.BlockSpec(
            (None, levels, block), lambda i: (field * bands + i // steps, 0, i % steps)
        )

    found = pl.pallas_call(
        cloud_kernel,
        grid=(bands * steps,),
        out_shape=jax.ShapeDtypeStruct((sections, bands, levels, span), jnp.float32),
        in_specs=[of(0), of(2), of(3), moist],
        out_specs=pl.BlockSpec(
            (sections, None, levels, block), lambda i: (0, i // steps, 0, i % steps)
        ),
        name="cloud",
    )(arrived, arrived, arrived, anomaly)
    return found.reshape(arrived.shape)


def halve(values):
    coarse = values.astype(jnp.bfloat16)
    return coarse, (values - coarse.astype(jnp.float32)).astype(jnp.bfloat16)


def march_kernel(
    grow_ref, retreat_ref, order_ref, zero_ref, cosine_ref, diag_ref, coarse_ref, fine_ref, *tables
):
    slots = order_ref.shape[0]
    halves = len(tables)
    order = order_ref[...]
    grow = grow_ref[...]
    retreat = retreat_ref[...]
    cosine = [cosine_ref[:, h * LANES : (h + 1) * LANES] for h in range(halves)]
    for h in range(halves):
        tables[h][: 2 * slots, :] = jnp.zeros((2 * slots, LANES), jnp.float32)
    group = 8

    def march(g, carry):
        begin = g * group
        held = [
            [
                tables[h][pl.ds(pl.multiple_of((begin + j) * slots, ROWS), slots), :]
                for j in range(2)
            ]
            for h in range(halves)
        ]
        for j in range(group):
            n = begin + j
            index = zero_ref[...] + n
            grow_n = jnp.take_along_axis(grow, index, axis=1)
            retreat_n = jnp.take_along_axis(retreat, index, axis=1)
            first = order == n
            for h in range(halves):
                previous, current = held[h]
                grown = grow_n * (cosine[h] * current - retreat_n * previous)
                fresh = jnp.where(first, diag_ref[:, h * LANES : (h + 1) * LANES], grown)
                tables[h][pl.ds(pl.multiple_of((n + 2) * slots, ROWS), slots), :] = fresh
                held[h] = [current, fresh]
        return carry

    lax.fori_loop(0, MMAX // group, march, 0)

    def sort(g, carry):
        for j in range(4):
            s = g * 4 + j
            for h in range(halves):
                rows = tables[h][pl.ds(2 * slots + s, MMAX, stride=slots), :]
                mine = slice(h * LANES, (h + 1) * LANES)
                coarse_ref[s, :, mine], fine_ref[s, :, mine] = halve(rows)
        return carry

    lax.fori_loop(0, slots // 4, sort, 0)


def contract_kernel(fourier_ref, coarse_ref, fine_ref, out_ref):
    levels, slots, _, _ = out_ref.shape
    bands = fourier_ref.shape[0]
    terms = 2 * levels
    rows = -(-terms // 16) * 16

    def product(left, right):
        return lax.dot_general(
            left, right, (((1,), (1,)), ((), ())), preferred_element_type=jnp.float32
        )

    def contract(g, carry):
        for j in range(4):
            s = g * 4 + j
            found = [fourier_ref[b, pl.ds(s, terms, stride=slots), :] for b in range(bands)]
            found = jnp.concatenate(found, axis=1)
            if rows > terms:
                fill = jnp.zeros((rows - terms, found.shape[1]), jnp.float32)
                found = jnp.concatenate([found, fill], axis=0)
            head, rest = halve(found)
            main = product(jnp.concatenate([head, rest], axis=0), coarse_ref[s])
            total = main[:rows] + main[rows:] + product(head, fine_ref[s])
            for l in range(levels):
                out_ref[l, s] = total[2 * l : 2 * l + 2]
        return carry

    lax.fori_loop(0, slots // 4, contract, 0)


def dft_kernel(x_ref, trig_ref, out_ref):
    blocks, levels, lats, _ = x_ref.shape
    parts, _, _, slots, lanes = out_ref.shape
    count = trig_ref.shape[1]
    waves = [jnp.concatenate(halve(trig_ref[j]), axis=0) for j in range(blocks)]

    def product(left, right):
        return lax.dot_general(
            left, right, (((1,), (1,)), ((), ())), preferred_element_type=jnp.float32
        )

    for first in range(0, levels, 2):
        last = min(first + 2, levels)
        total = None
        for j in range(blocks):
            grid = []
            for l in range(first, last):
                grid.append(x_ref[j, l])
                if lanes > lats:
                    grid.append(jnp.zeros((lanes - lats, x_ref.shape[3]), jnp.float32))
            coarse, fine = halve(jnp.concatenate(grid, axis=0))
            main = product(waves[j], coarse)
            term = main[:count] + main[count:] + product(waves[j][:count], fine)
            total = term if total is None else total + term
        for l in range(first, last):
            mine = total[:, (l - first) * lanes : (l - first + 1) * lanes]
            for p in range(parts):
                for c in range(2):
                    begin = (p * 2 + c) * slots
                    out_ref[p, l, c] = mine[begin : begin + slots]


def dft(regrouped, wave_table, blocks, parts):
    _, lats, lons = regrouped.shape
    levels = regrouped.shape[0] // blocks
    slots = wave_table.shape[0] // parts
    pad = -lats % ROWS
    lanes = -(-lats // LANES) * LANES
    grid = jnp.pad(regrouped, ((0, 0), (0, pad), (0, 0)))
    trig = trig_table(jnp.arange(NLON, dtype=jnp.int32), wave_table)
    trig = trig.reshape(blocks, lons, 2, parts, slots).transpose(0, 3, 2, 4, 1)
    return pl.pallas_call(
        dft_kernel,
        out_shape=jax.ShapeDtypeStruct((parts, levels, 2, slots, lanes), jnp.float32),
        in_specs=[pl.BlockSpec(memory_space=pltpu.VMEM)] * 2,
        out_specs=pl.BlockSpec(memory_space=pltpu.VMEM),
        name="dft",
    )(
        grid.reshape(blocks, levels, lats + pad, lons),
        trig.reshape(blocks, 2 * parts * slots, lons),
    )


def legendre_tables(orders, lats, bands):
    slots = orders.shape[0]
    wide = bands * (-(-(lats // bands) // LANES) * LANES)
    colatitude = (jnp.arange(lats, dtype=jnp.int32).astype(jnp.float32) + 0.5) * (math.pi / lats)
    sine_lat = jnp.sin(colatitude)
    order_col = orders.astype(jnp.float32)[:, None]
    log_diag = 0.5 * (
        lax.lgamma(order_col + 1.5) - lax.lgamma(jnp.float32(1.5)) - lax.lgamma(order_col + 1.0)
    )
    log_diag = log_diag + order_col * jnp.log(sine_lat)[None, :] - 0.5 * math.log(2.0)
    diagonal = jnp.exp(log_diag) * (sine_lat / math.sqrt(lats))[None, :]
    degree = jnp.arange(MMAX, dtype=jnp.int32).astype(jnp.float32)[None, :]
    active = degree > order_col
    numerator = jnp.where(active, 4.0 * degree * degree - 1.0, 0.0)
    bottom = jnp.where(active, degree * degree - order_col * order_col, 1.0)
    lower = degree - 1.0
    retreat = jnp.sqrt(
        jnp.maximum(lower * lower - order_col * order_col, 0.0) / (4.0 * lower * lower - 1.0)
    )
    grow = jnp.sqrt(numerator / bottom)

    def spread(values):
        cut = values.reshape(values.shape[0], bands, lats // bands)
        cut = jnp.pad(cut, ((0, 0), (0, 0), (0, wide // bands - lats // bands)))
        return cut.reshape(values.shape[0], wide)

    table = jax.ShapeDtypeStruct((slots, MMAX, wide), jnp.bfloat16)
    return pl.pallas_call(
        march_kernel,
        out_shape=[table] * 2,
        in_specs=[pl.BlockSpec(memory_space=pltpu.VMEM)] * 6,
        out_specs=[pl.BlockSpec(memory_space=pltpu.VMEM)] * 2,
        scratch_shapes=[pltpu.VMEM(((MMAX + 2) * slots, LANES), jnp.float32)] * (wide // LANES),
        cost_estimate=pl.CostEstimate(
            flops=6 * MMAX * slots * wide, bytes_accessed=16 * MMAX * slots * wide, transcendentals=0
        ),
        name="march",
    )(
        grow,
        retreat,
        jnp.broadcast_to(orders[:, None], (slots, LANES)),
        jnp.zeros((slots, LANES), jnp.int32),
        spread(jnp.cos(colatitude)[None, :]),
        spread(diagonal),
    )


def contract_tables(fourier, tables):
    bands, levels, _, slots, lanes = fourier.shape
    return pl.pallas_call(
        contract_kernel,
        out_shape=jax.ShapeDtypeStruct((levels, slots, 2, MMAX), jnp.float32),
        in_specs=[pl.BlockSpec(memory_space=pltpu.VMEM)] * 3,
        out_specs=pl.BlockSpec(memory_space=pltpu.VMEM),
        name="contract",
    )(fourier.reshape(bands, levels * 2 * slots, lanes), *tables)


def trig_table(longitudes, wave_numbers):
    phase = (longitudes[:, None] * wave_numbers[None, :] % NLON).astype(jnp.float32) * (
        2.0 * math.pi / NLON
    )
    return jnp.stack((jnp.cos(phase), jnp.sin(phase)), axis=1) / math.sqrt(NLON)


def inverse_order(order):
    cols = order.shape[0]
    tiles = cols // LANES
    slots = jnp.arange(cols, dtype=jnp.int32)
    high = (order[None, :] // LANES) == jnp.arange(tiles, dtype=jnp.int32)[:, None]
    low = (order[:, None] % LANES) == jnp.arange(LANES, dtype=jnp.int32)[None, :]
    digits = jnp.stack((slots // LANES, slots % LANES)).astype(jnp.bfloat16)
    left = jnp.where(high[None], digits[:, None, :], jnp.bfloat16(0)).reshape(2 * tiles, cols)
    found = jnp.dot(left, low.astype(jnp.bfloat16), preferred_element_type=jnp.float32)
    found = found.reshape(2, cols).astype(jnp.int32)
    return found[0] * LANES + found[1]


def shards(state, forcing, crm_moisture, cloud_order, wave_table):
    members, _, levels, band_rows, lon_block = state.shape
    sections = lax.axis_size("sec")
    lat_bands = lax.axis_size("lat")
    block_cols = band_rows * lon_block
    targets = sections * lat_bands
    per_target = block_cols // targets
    field = lax.axis_index("sec")
    slot_list = cloud_order[0, 0]
    own, force = state[0, 0], forcing[0, 0]

    mate = lax.ppermute(jnp.where(field == 2, force, own), "sec", [(2, 3), (3, 2)])
    part = jnp.where(
        field == 3, (force - mate) / NSUB, jnp.where(field == 2, mate - own, own)
    )
    flat = part.reshape(levels, block_cols)
    cut = (targets, levels, per_target)
    tiled = per_target % LANES == 0
    if tiled:
        outgoing = permute(flat, slot_list[None, :], cut)
    else:
        in_slots = permute(flat, slot_list[None, :], flat.shape)
        outgoing = in_slots.reshape(levels, targets, per_target).transpose(1, 0, 2)
    crm_moisture, outgoing = lax.optimization_barrier((crm_moisture, outgoing))
    arrived = lax.all_to_all(outgoing, ("sec", "lat"), split_axis=0, concat_axis=0, tiled=True)
    homeward = cloud_model(arrived, crm_moisture[0, :, :, 0, 0, :], sections)
    returned = lax.all_to_all(homeward, ("sec", "lat"), split_axis=0, concat_axis=0, tiled=True)
    if not tiled:
        returned = returned.transpose(1, 0, 2).reshape(levels, block_cols)
    rainfall = permute(returned, inverse_order(slot_list)[None, :], flat.shape)
    rainfall = rainfall.reshape(levels, band_rows, lon_block)
    share = jnp.where(
        field < 2, own * (-1.0 / NSUB), jnp.where(field == 2, jnp.float32(1), jnp.float32(-1))
    )
    fresh = own + (share * rainfall + force)

    regrouped = lax.all_to_all(fresh, "col", split_axis=0, concat_axis=0, tiled=True)
    owner_count = MMAX // lat_bands
    wave_table, _ = lax.optimization_barrier((wave_table, rainfall))
    owned_waves = lax.dynamic_slice_in_dim(
        wave_table, lax.axis_index("lat") * owner_count, owner_count
    )
    tables = legendre_tables(owned_waves, NLAT, lat_bands)
    regrouped, tables = lax.optimization_barrier((regrouped, tables))
    spectra = dft(regrouped, wave_table, lax.axis_size("col"), lat_bands)
    gathered = lax.all_to_all(spectra, "lat", split_axis=0, concat_axis=0, tiled=True)
    coeffs = contract_tables(gathered, tables)
    return (fresh[None, None], coeffs[None, None])


def solution(mesh):
    placed = (
        P(None, "sec", None, "lat", "col"),
        P(None, "sec", None, "lat", "col"),
        P(None, None, None, ("sec", "lat"), "col", None),
        P("col", "lat", None),
        P(),
    )
    return jax.shard_map(
        shards,
        mesh=mesh,
        in_specs=placed,
        out_specs=(P(None, "sec", None, "lat", "col"), P("sec", None, "col", "lat", None, None)),
        check_vma=False,
    )
```

profile of v0, /device:TPU:0, one launch (start us, length us, event | category | flops | bytes accessed | tf_op | source)
XLA Modules:
  0.0 178.4 jit_solution(9728323830269053248)
XLA Ops:
  0.7 3.1 %bitcast_select_fusion = f32[28,96,96]{2,1,0:T(8,128)} fusion(f32[1,1,28,96,96]{4,3,2,1,0:T(8,128)} %param.5, f32[1,1,28,96,96]{4,3,2,1,0:T(8,128)} %param.6, pred[]{:T(512)S(6)} %eq.44), kind=kLoop, calls=%fused_computation.10 | loop fusion | flops 258048 | bytes 3096577 | tf_op jit(solution)/shard_map/jit(_where)/select_n | solution.py:399
  3.8 1.8 collective-permute-start
  5.6 0.7 add_select_fusion.1
  6.7 2.8 %fusion.2 = f32[28,96,96]{2,1,0:T(8,128)} fusion(f32[28,96,96]{2,1,0:T(8,128)} %collective-permute-done, f32[1,1,28,96,96]{4,3,2,1,0:T(8,128)S(1)} %copy-done, f32[1,1,28,96,96]{4,3,2,1,0:T(8,128)S(1)} %copy-done.1, pred[]{:T(512)S(6)} %eq.44, pred[]{:T(512)S(6)} %eq.45), kind=kLoop, calls=%fused_computation.7 | loop fusion | flops 1290240 | bytes 4128770 | tf_op jit(solution)/shard_map/jit(_where)/select_n | solution.py:400
  9.5 3.2 %reshape.490.x_ref = f32[28,9216]{1,0:T(8,128)} reshape(f32[28,96,96]{2,1,0:T(8,128)} %fusion.2) | data formatting | bytes 2064384 | tf_op jit(solution)/shard_map/reshape | solution.py:403
  12.7 16.7 %permute.2 = f32[8,28,1152]{2,1,0:T(8,128)} custom-call(f32[28,9216]{1,0:T(8,128)} %reshape.490.x_ref, s32[1,9216]{1,0:T(1,128)} %bitcast.48), custom_call_target="tpu_custom_call" | custom-call | tf_op jit(solution)/shard_map/permute/pallas_call | solution.py:91
  29.4 7.7 %all-to-all-start = ((f32[8,28,1152]{2,1,0:T(8,128)}), f32[8,28,1152]{2,1,0:T(8,128)}, u32[]{:S(2)}, u32[]{:S(2)}) async-start(f32[8,28,1152]{2,1,0:T(8,128)} %permute.2), calls=%async_computation | async-start | bytes 2359296 | tf_op jit(solution)/shard_map/all_to_all | solution.py:412
  37.2 6.6 %copy.11 = bf16[1,32,28,1,1,2304]{5,2,1,4,3,0:T(8,128)(2,1)} copy(bf16[1,32,28,1,1,2304]{5,1,4,3,2,0:T(8,128)(2,1)} %param.7) | data formatting | bytes 8257536 | tf_op jit(solution)/shard_map/optimization_barrier | solution.py:411
  43.8 9.3 %all-to-all-done.wind_ref.gap_ref.push_ref = f32[8,28,1152]{2,1,0:T(8,128)} async-done(((f32[8,28,1152]{2,1,0:T(8,128)}), f32[8,28,1152]{2,1,0:T(8,128)}, u32[]{:S(2)}, u32[]{:S(2)}) %all-to-all-start) | async-done | bytes 1032224 | tf_op jit(solution)/shard_map/all_to_all | solution.py:412
  53.1 15.7 %cloud.1 = f32[4,2,28,1152]{3,2,1,0:T(8,128)} custom-call(f32[8,28,1152]{2,1,0:T(8,128)} %all-to-all-done.wind_ref.gap_ref.push_ref, f32[8,28,1152]{2,1,0:T(8,128)} %all-to-all-done.wind_ref.gap_ref.push_ref, f32[8,28,1152]{2,1,0:T(8,128)} %all-to-all-done.wind_ref.gap_ref.push_ref, bf16[32,28,2304]{2,1,0:T(8,128)(2,1)} %bitcast.41), custom_call_target="tpu_custom_call" | custom-call | tf_op jit(solution)/shard_map/cloud/pallas_call | solution.py:160
  68.8 4.3 %all-to-all-start.1 = ((f32[8,28,1152]{2,1,0:T(8,128)}), f32[8,28,1152]{2,1,0:T(8,128)}, u32[]{:S(2)}, u32[]{:S(2)}) async-start(f32[8,28,1152]{2,1,0:T(8,128)} %bitcast.42), calls=%async_computation.1 | async-start | bytes 2359296 | tf_op jit(solution)/shard_map/all_to_all | solution.py:414
  73.1 2.0 %broadcast_select_fusion = bf16[2,72,9216]{2,1,0:T(8,128)(2,1)} fusion(pred[72,9216]{1,0:T(8,128)(4,1)S(1)} %iota_compare_fusion.2, bf16[2,9216]{1,0:T(2,128)(2,1)S(1)} %pad_maximum_fusion), kind=kLoop, calls=%fused_computation.4 | loop fusion | flops 1327104 | bytes 3354624 | tf_op jit(solution)/shard_map/jit(_where)/select_n | solution.py:382
  75.7 6.5 %fusion.7 = s32[144,128]{1,0:T(8,128)S(1)} fusion(bf16[144,9216]{1,0:T(8,128)(2,1)} %bitcast.43, s32[9216]{0:T(1024)S(1)} %copy-done.3), kind=kOutput, calls=%fused_computation.17 | convolution fusion | flops 340936704 | bytes 2764800 | tf_op jit(solution)/shard_map/dot_general | solution.py:383
  82.2 0.6 slice_add_fusion
  82.8 6.2 %all-to-all-done.1.x_ref = f32[8,28,1152]{2,1,0:T(8,128)} async-done(((f32[8,28,1152]{2,1,0:T(8,128)}), f32[8,28,1152]{2,1,0:T(8,128)}, u32[]{:S(2)}, u32[]{:S(2)}) %all-to-all-start.1) | async-done | bytes 1032224 | tf_op jit(solution)/shard_map/all_to_all | solution.py:414
  89.0 16.7 %permute.3 = f32[28,9216]{1,0:T(8,128)} custom-call(f32[8,28,1152]{2,1,0:T(8,128)} %all-to-all-done.1.x_ref, s32[1,9216]{1,0:T(1,128)} %bitcast.50), custom_call_target="tpu_custom_call" | custom-call | tf_op jit(solution)/shard_map/permute/pallas_call | solution.py:91
  105.7 2.9 %reshape.493 = f32[28,96,96]{2,1,0:T(8,128)} reshape(f32[28,9216]{1,0:T(8,128)} %permute.3) | data formatting | bytes 2064384 | tf_op jit(solution)/shard_map/reshape | solution.py:418
  108.6 2.8 %bitcast_add_fusion = f32[28,96,96]{2,1,0:T(8,128)} fusion(f32[1,1,28,96,96]{4,3,2,1,0:T(8,128)S(1)} %copy-done, f32[28,96,96]{2,1,0:T(8,128)} %reshape.493, f32[1,1,28,96,96]{4,3,2,1,0:T(8,128)S(1)} %copy-done.1, f32[]{:T(128)S(6)} %select_n.125, pred[]{:T(512)S(6)} %lt.24), kind=kLoop, calls=%fused_computation.9 | loop fusion | flops 1290240 | bytes 4128773 | tf_op jit(solution)/shard_map/add | solution.py:422
  111.4 5.0 %all-to-all-start.2 = ((f32[28,96,96]{2,1,0:T(8,128)}), f32[28,96,96]{2,1,0:T(8,128)}, u32[]{:S(2)}, u32[]{:S(2)}) async-start(f32[28,96,96]{2,1,0:T(8,128)} %bitcast_add_fusion), calls=%async_computation.2 | async-start | bytes 2752512 | tf_op jit(solution)/shard_map/all_to_all | solution.py:424
  116.9 0.6 copy.12
  117.6 0.7 divide_sqrt_fusion
  118.3 0.7 broadcast_in_dim.74.order_ref
  119.6 19.3 %march.1 = (bf16[64,128,256]{2,1,0:T(8,128)(2,1)}, bf16[64,128,256]{2,1,0:T(8,128)(2,1)}) custom-call(f32[64,128]{1,0:T(8,128)} %get-tuple-element.25.grow_ref, f32[64,128]{1,0:T(8,128)} %get-tuple-element.24.retreat_ref, s32[64,128]{1,0:T(8,128)} %broadcast_in_dim.74.order_ref, s32[64,128]{1,0:T(8,128)} %broadcast_in_dim.75.zero_ref, f32[1,256]{1,0:T(1,128)} %bitcast.51, ...), custom_call_target="tpu_custom_call" | custom-call | flops 12582912 | bytes 33554432 | tf_op jit(solution)/shard_map/march/pallas_call | solution.py:337
  138.9 1.1 fusion.13
  140.1 0.9 maximum_multiply_fusion
  141.0 8.4 %all-to-all-done.2 = f32[28,96,96]{2,1,0:T(8,128)} async-done(((f32[28,96,96]{2,1,0:T(8,128)}), f32[28,96,96]{2,1,0:T(8,128)}, u32[]{:S(2)}, u32[]{:S(2)}) %all-to-all-start.2) | async-done | bytes 1032224 | tf_op jit(solution)/shard_map/all_to_all | solution.py:424
  149.4 4.0 %dft.1 = f32[2,7,2,64,128]{4,3,2,1,0:T(8,128)} custom-call(f32[4,7,96,96]{3,2,1,0:T(8,128)} %bitcast.9.x_ref, f32[4,256,96]{2,1,0:T(8,128)} %bitcast.44), custom_call_target="tpu_custom_call" | custom-call | tf_op jit(solution)/shard_map/dft/pallas_call | solution.py:298
  153.4 4.4 %all-to-all-start.3 = ((f32[2,7,2,64,128]{4,3,2,1,0:T(8,128)}), f32[2,7,2,64,128]{4,3,2,1,0:T(8,128)}, u32[]{:S(2)}, u32[]{:S(2)}) async-start(f32[2,7,2,64,128]{4,3,2,1,0:T(8,128)} %dft.1), calls=%async_computation.3 | async-start | bytes 1835008 | tf_op jit(solution)/shard_map/all_to_all | solution.py:433
  157.8 2.9 %reshape.492 = f32[1,1,28,96,96]{4,3,2,1,0:T(8,128)} reshape(f32[28,9216]{1,0:T(8,128)} %permute.3) | data formatting | bytes 2064384 | tf_op jit(solution)/shard_map/reshape | solution.py:418
  160.7 2.8 %add_add_fusion = f32[1,1,28,96,96]{4,3,2,1,0:T(8,128)} fusion(f32[1,1,28,96,96]{4,3,2,1,0:T(8,128)S(1)} %copy-done, f32[1,1,28,96,96]{4,3,2,1,0:T(8,128)S(1)} %copy-done.1, f32[1,1,28,96,96]{4,3,2,1,0:T(8,128)} %reshape.492, f32[]{:T(128)S(6)} %select_n.125, pred[]{:T(512)S(6)} %lt.24), kind=kLoop, calls=%fused_computation.16 | loop fusion | flops 1290240 | bytes 4128773 | tf_op jit(solution)/shard_map/add | solution.py:422
  163.5 6.1 %all-to-all-done.3 = f32[2,7,2,64,128]{4,3,2,1,0:T(8,128)} async-done(((f32[2,7,2,64,128]{4,3,2,1,0:T(8,128)}), f32[2,7,2,64,128]{4,3,2,1,0:T(8,128)}, u32[]{:S(2)}, u32[]{:S(2)}) %all-to-all-start.3) | async-done | bytes 917536 | tf_op jit(solution)/shard_map/all_to_all | solution.py:433
  169.6 8.8 %contract.1 = f32[7,64,2,128]{3,2,1,0:T(2,128)} custom-call(f32[2,896,128]{2,1,0:T(8,128)} %bitcast.12.fourier_ref, bf16[64,128,256]{2,1,0:T(8,128)(2,1)} %get-tuple-element.16.coarse_ref, bf16[64,128,256]{2,1,0:T(8,128)(2,1)} %get-tuple-element.17.fine_ref), custom_call_target="tpu_custom_call" | custom-call | tf_op jit(solution)/shard_map/contract/pallas_call | solution.py:359
  (28 shorter events, 2.3 us)
Async XLA Ops:
  0.6 4.9 %copy-start.2 = (s32[1,1,9216]{2,1,0:T(1,128)S(1)}, s32[1,1,9216]{2,1,0:T(1,128)}, u32[]{:S(2)}) copy-start(s32[1,1,9216]{2,1,0:T(1,128)} %param.8) | copy-start | bytes 110596
  0.6 6.0 %copy-start = (f32[1,1,28,96,96]{4,3,2,1,0:T(8,128)S(1)}, f32[1,1,28,96,96]{4,3,2,1,0:T(8,128)}, u32[]{:S(2)}) copy-start(f32[1,1,28,96,96]{4,3,2,1,0:T(8,128)} %param.5) | copy-start | bytes 3096580
  0.7 6.0 %copy-start.1 = (f32[1,1,28,96,96]{4,3,2,1,0:T(8,128)S(1)}, f32[1,1,28,96,96]{4,3,2,1,0:T(8,128)}, u32[]{:S(2)}) copy-start(f32[1,1,28,96,96]{4,3,2,1,0:T(8,128)} %param.6) | copy-start | bytes 3096580
  3.8 2.9 %collective-permute-start = (f32[28,96,96]{2,1,0:T(8,128)}, f32[28,96,96]{2,1,0:T(8,128)}, u32[]{:S(2)}, u32[]{:S(2)}) collective-permute-start(f32[28,96,96]{2,1,0:T(8,128)} %bitcast_select_fusion), channel_id=1, source_target_pairs={{16,24},{24,16},{17,25},{25,17},{18,26},{26,18},{19,27},{27,19},{2... | collective-permute-start | bytes 3096584 | tf_op jit(solution)/shard_map/ppermute | solution.py:399
  29.4 23.7 %all-to-all-start = ((f32[8,28,1152]{2,1,0:T(8,128)}), f32[8,28,1152]{2,1,0:T(8,128)}, u32[]{:S(2)}, u32[]{:S(2)}) async-start(f32[8,28,1152]{2,1,0:T(8,128)} %permute.2), calls=%async_computation | async-start | bytes 2359296 | tf_op jit(solution)/shard_map/all_to_all | solution.py:412
  68.8 20.2 %all-to-all-start.1 = ((f32[8,28,1152]{2,1,0:T(8,128)}), f32[8,28,1152]{2,1,0:T(8,128)}, u32[]{:S(2)}, u32[]{:S(2)}) async-start(f32[8,28,1152]{2,1,0:T(8,128)} %bitcast.42), calls=%async_computation.1 | async-start | bytes 2359296 | tf_op jit(solution)/shard_map/all_to_all | solution.py:414
  73.0 2.6 %copy-start.3 = (s32[9216]{0:T(1024)S(1)}, s32[9216]{0:T(1024)}, u32[]{:S(2)}) copy-start(s32[9216]{0:T(1024)} %get-tuple-element.20) | copy-start | bytes 110596
  111.4 5.1 %copy-start.4 = (s32[128]{0:T(128)S(1)}, s32[128]{0:T(128)}, u32[]{:S(2)}) copy-start(s32[128]{0:T(128)} %param.9) | copy-start | bytes 1540
  111.4 38.0 %all-to-all-start.2 = ((f32[28,96,96]{2,1,0:T(8,128)}), f32[28,96,96]{2,1,0:T(8,128)}, u32[]{:S(2)}, u32[]{:S(2)}) async-start(f32[28,96,96]{2,1,0:T(8,128)} %bitcast_add_fusion), calls=%async_computation.2 | async-start | bytes 2752512 | tf_op jit(solution)/shard_map/all_to_all | solution.py:424
  153.4 16.2 %all-to-all-start.3 = ((f32[2,7,2,64,128]{4,3,2,1,0:T(8,128)}), f32[2,7,2,64,128]{4,3,2,1,0:T(8,128)}, u32[]{:S(2)}, u32[]{:S(2)}) async-start(f32[2,7,2,64,128]{4,3,2,1,0:T(8,128)} %dft.1), calls=%async_computation.3 | async-start | bytes 1835008 | tf_op jit(solution)/shard_map/all_to_all | solution.py:433
where the time goes:
time: 180 us; the launch traced here: 178 us
  Pallas kernels  81.2 us (45%)
  waiting for transfers between devices  30.1 us (17%)
  starting transfers between devices  23.1 us (13%)
  other arithmetic  18.5 us (10%)
  local copies, waits for them, and re-layouts  18.3 us (10%)
  matrix products  6.52 us (4%)
    pallas_call x2, Pallas kernels, permute(): pl.pallas_call(permute_kernel, out_shape=jax.ShapeDtypeStruct(shape, jnp....  33.4 us
    pallas_call x1, Pallas kernels, legendre_tables(): pl.pallas_call(march_kernel, out_shape=[table] * 2, in_specs=[pl.BlockSpe...  19.3 us
    pallas_call x1, Pallas kernels, cloud_model(): pl.pallas_call(cloud_kernel, grid=(bands * steps,), out_shape=jax.ShapeDt...  15.7 us
    all_to_all x1, waiting for transfers between devices, shards(): lax.all_to_all(outgoing, ('sec', 'lat'), split_axis=0, concat_axis=0, til...  9.34 us
    pallas_call x1, Pallas kernels, contract_tables(): pl.pallas_call(contract_kernel, out_shape=jax.ShapeDtypeStruct((levels, s...  8.82 us
    all_to_all x1, waiting for transfers between devices, shards(): lax.all_to_all(fresh, 'col', split_axis=0, concat_axis=0, tiled=True)  8.44 us
    all_to_all x1, starting transfers between devices, shards(): lax.all_to_all(outgoing, ('sec', 'lat'), split_axis=0, concat_axis=0, til...  7.69 us
    optimization_barrier x1, local copies, waits for them, and re-layouts, shards(): crm_moisture, outgoing = lax.optimization_barrier((crm_moisture, outgoing))  6.6 us
  transfers between devices with their start and end apart: 5, of which 4 were waited for; matrix products, arithmetic and copies ran while one was open for 16% of the time, Pallas kernels for 11%

commit v1 on v0

--- a/solution.py
+++ b/solution.py
@@ -307,9 +307,7 @@
     )
 
 
-def legendre_tables(orders, lats, bands):
-    slots = orders.shape[0]
-    wide = bands * (-(-(lats // bands) // LANES) * LANES)
+def legendre_terms(orders, lats):
     colatitude = (jnp.arange(lats, dtype=jnp.int32).astype(jnp.float32) + 0.5) * (math.pi / lats)
     sine_lat = jnp.sin(colatitude)
     order_col = orders.astype(jnp.float32)[:, None]
@@ -326,7 +324,13 @@
     retreat = jnp.sqrt(
         jnp.maximum(lower * lower - order_col * order_col, 0.0) / (4.0 * lower * lower - 1.0)
     )
-    grow = jnp.sqrt(numerator / bottom)
+    return jnp.sqrt(numerator / bottom), retreat, jnp.cos(colatitude), diagonal
+
+
+def legendre_tables(orders, lats, bands):
+    slots = orders.shape[0]
+    wide = bands * (-(-(lats // bands) // LANES) * LANES)
+    grow, retreat, cosine, diagonal = legendre_terms(orders, lats)
 
     def spread(values):
         cut = values.reshape(values.shape[0], bands, lats // bands)
@@ -349,7 +353,7 @@
         retreat,
         jnp.broadcast_to(orders[:, None], (slots, LANES)),
         jnp.zeros((slots, LANES), jnp.int32),
-        spread(jnp.cos(colatitude)[None, :]),
+        spread(cosine[None, :]),
         spread(diagonal),
     )
 
@@ -370,6 +374,242 @@
         2.0 * math.pi / NLON
     )
     return jnp.stack((jnp.cos(phase), jnp.sin(phase)), axis=1) / math.sqrt(NLON)
+
+
+MESH_IDS = pl.DeviceIdType.MESH
+
+
+def lanes_product(left, right):
+    return lax.dot_general(
+        left, right, (((1,), (1,)), ((), ())), preferred_element_type=jnp.float32
+    )
+
+
+def march(grow, retreat, order, zero, cosine, diag_ref, table, coarse_ref, fine_ref):
+    slots = order.shape[0]
+    table[: 2 * slots, :] = jnp.zeros((2 * slots, LANES), jnp.float32)
+    group = 8
+
+    def degrees(g, carry):
+        begin = g * group
+        previous, current = [
+            table[pl.ds(pl.multiple_of((begin + j) * slots, ROWS), slots), :] for j in range(2)
+        ]
+        for j in range(group):
+            n = begin + j
+            index = zero + n
+            grow_n = jnp.take_along_axis(grow, index, axis=1)
+            retreat_n = jnp.take_along_axis(retreat, index, axis=1)
+            grown = grow_n * (cosine * current - retreat_n * previous)
+            fresh = jnp.where(order == n, diag_ref[...], grown)
+            table[pl.ds(pl.multiple_of((n + 2) * slots, ROWS), slots), :] = fresh
+            previous, current = current, fresh
+        return carry
+
+    lax.fori_loop(0, MMAX // group, degrees, 0)
+
+    def sort(g, carry):
+        for j in range(4):
+            s = g * 4 + j
+            rows = table[pl.ds(2 * slots + s, MMAX, stride=slots), :]
+            coarse_ref[s], fine_ref[s] = halve(rows)
+        return carry
+
+    lax.fori_loop(0, slots // 4, sort, 0)
+
+
+def spectral_kernel(
+    fresh_ref,
+    trig_ref,
+    grow_ref,
+    retreat_ref,
+    order_ref,
+    zero_ref,
+    cosine_ref,
+    diag_ref,
+    out_ref,
+    zbuf,
+    ybuf,
+    ystage,
+    wave_coarse,
+    wave_fine,
+    table,
+    coarse,
+    fine,
+    both,
+    local_sem,
+    zsend,
+    zrecv,
+    ysend,
+    yrecv,
+):
+    cols = lax.axis_size("col")
+    col, lat = lax.axis_index("col"), lax.axis_index("lat")
+    levels, lats = zbuf.shape[1], zbuf.shape[2]
+    slots = order_ref.shape[0]
+    partner = 1 - lat
+
+    barrier = pltpu.get_barrier_semaphore()
+    for d in range(1, cols):
+        pl.semaphore_signal(
+            barrier, inc=1, device_id={"col": lax.rem(col + d, cols)}, device_id_type=MESH_IDS
+        )
+    pl.semaphore_signal(barrier, inc=1, device_id={"lat": partner}, device_id_type=MESH_IDS)
+    own = pltpu.make_async_copy(
+        fresh_ref.at[pl.ds(col * levels, levels)], zbuf.at[col], local_sem
+    )
+    own.start()
+    pl.semaphore_wait(barrier, cols)
+
+    def zcopy(l, d):
+        dest = lax.rem(col + d, cols)
+        return pltpu.make_async_remote_copy(
+            src_ref=fresh_ref.at[dest * levels + l],
+            dst_ref=zbuf.at[col, l],
+            send_sem=zsend.at[l, d - 1],
+            recv_sem=zrecv.at[l, d - 1],
+            device_id={"col": dest},
+            device_id_type=MESH_IDS,
+        )
+
+    for l in range(levels):
+        for d in range(1, cols):
+            zcopy(l, d).start()
+
+    for j in range(cols):
+        wave_coarse[j], wave_fine[j] = halve(trig_ref[j])
+    march(
+        grow_ref[...],
+        retreat_ref[...],
+        order_ref[...],
+        zero_ref[...],
+        cosine_ref[...],
+        diag_ref,
+        table,
+        coarse,
+        fine,
+    )
+    own.wait()
+
+    def ycopy(l):
+        return pltpu.make_async_remote_copy(
+            src_ref=ystage.at[l],
+            dst_ref=ybuf.at[lat, l],
+            send_sem=ysend.at[l],
+            recv_sem=yrecv.at[l],
+            device_id={"lat": partner},
+            device_id_type=MESH_IDS,
+        )
+
+    def transform(l, carry):
+        for d in range(1, cols):
+            zcopy(l, d).wait_recv()
+        total = None
+        for j in range(cols):
+            head, rest = halve(zbuf[j, l])
+            main = lanes_product(jnp.concatenate([head, rest], axis=0), wave_coarse[j])
+            term = main[:lats] + main[lats:] + lanes_product(head, wave_fine[j])
+            total = term if total is None else total + term
+        ybuf[lat, l] = total[:, : 2 * slots]
+        ystage[l] = total[:, 2 * slots :]
+        ycopy(l).start()
+        return carry
+
+    lax.fori_loop(0, levels, transform, 0)
+
+    lane = lax.broadcasted_iota(jnp.int32, (2 * slots, LANES), 1)
+    mirror = jnp.where(lane < lats, lats - 1 - lane, lane)
+    fill = jnp.zeros((2 * slots, LANES - lats), jnp.float32)
+    both[...] = jnp.zeros_like(both)
+    span = both.shape[0] // 2
+
+    def mix(l, carry):
+        ycopy(l).wait_recv()
+        north = jnp.concatenate([ybuf[0, l].T, fill], axis=1)
+        south = jnp.concatenate([ybuf[1, l].T, fill], axis=1)
+        south = jnp.take_along_axis(south, mirror, axis=1)
+        at = pl.ds(pl.multiple_of(l * 2 * slots, ROWS), 2 * slots)
+        both[at, :] = north + south
+        at = pl.ds(pl.multiple_of(span + l * 2 * slots, ROWS), 2 * slots)
+        both[at, :] = north - south
+        return carry
+
+    lax.fori_loop(0, levels, mix, 0)
+    half = both.shape[0] // slots // 2
+    degree = lax.broadcasted_iota(jnp.int32, (half, LANES), 1)
+
+    def contract(g, carry):
+        for j in range(4):
+            s = g * 4 + j
+            head, rest = halve(both[pl.ds(s, 2 * half, stride=slots), :])
+            main = lanes_product(jnp.concatenate([head, rest], axis=0), coarse[s])
+            total = main[: 2 * half] + main[2 * half :] + lanes_product(head, fine[s])
+            even = ((order_ref[pl.ds(s, 1), :] + degree) & 1) == 0
+            total = jnp.where(even, total[:half], total[half:])
+            for l in range(levels):
+                out_ref[l, s] = total[2 * l : 2 * l + 2]
+        return carry
+
+    lax.fori_loop(0, slots // 4, contract, 0)
+
+    def drain(l, carry):
+        for d in range(1, cols):
+            zcopy(l, d).wait_send()
+        ycopy(l).wait_send()
+        return carry
+
+    lax.fori_loop(0, levels, drain, 0)
+
+
+def spectral_step(fresh, wave_table):
+    cols, lat_bands = lax.axis_size("col"), lax.axis_size("lat")
+    total_levels, band_rows, lon_block = fresh.shape
+    levels = total_levels // cols
+    slots = MMAX // lat_bands
+    lat = lax.axis_index("lat")
+    waves = lax.dynamic_slice_in_dim(
+        jnp.concatenate([wave_table, wave_table]), lat * slots, lat_bands * slots
+    )
+    trig = trig_table(jnp.arange(NLON, dtype=jnp.int32), waves)
+    trig = trig.reshape(cols, lon_block, 2, lat_bands, slots).transpose(0, 3, 2, 4, 1)
+    trig = trig.reshape(cols, lat_bands * 2 * slots, lon_block)
+    grow, retreat, cosine, diagonal = legendre_terms(waves[:slots], NLAT)
+    pad = ((0, 0), (0, LANES - band_rows))
+    vmem = pl.BlockSpec(memory_space=pltpu.VMEM)
+    half = -(-2 * levels // ROWS) * ROWS
+    return pl.pallas_call(
+        spectral_kernel,
+        out_shape=jax.ShapeDtypeStruct((levels, slots, 2, MMAX), jnp.float32),
+        in_specs=[pl.BlockSpec(memory_space=pl.ANY)] + [vmem] * 7,
+        out_specs=vmem,
+        scratch_shapes=[
+            pltpu.VMEM((cols, levels, band_rows, lon_block), jnp.float32),
+            pltpu.VMEM((lat_bands, levels, band_rows, 2 * slots), jnp.float32),
+            pltpu.VMEM((levels, band_rows, 2 * slots), jnp.float32),
+            pltpu.VMEM(trig.shape, jnp.bfloat16),
+            pltpu.VMEM(trig.shape, jnp.bfloat16),
+            pltpu.VMEM(((MMAX + 2) * slots, LANES), jnp.float32),
+            pltpu.VMEM((slots, MMAX, LANES), jnp.bfloat16),
+            pltpu.VMEM((slots, MMAX, LANES), jnp.bfloat16),
+            pltpu.VMEM((2 * half * slots, LANES), jnp.float32),
+            pltpu.SemaphoreType.DMA,
+            pltpu.SemaphoreType.DMA((levels, cols - 1)),
+            pltpu.SemaphoreType.DMA((levels, cols - 1)),
+            pltpu.SemaphoreType.DMA((levels,)),
+            pltpu.SemaphoreType.DMA((levels,)),
+        ],
+        compiler_params=pltpu.CompilerParams(collective_id=1, has_side_effects=True),
+        name="spectral",
+    )(
+        fresh,
+        trig,
+        grow,
+        retreat,
+        jnp.broadcast_to(waves[:slots, None], (slots, LANES)),
+        jnp.zeros((slots, LANES), jnp.int32),
+        jnp.pad(cosine[None, :band_rows], pad),
+        jnp.pad(diagonal[:, :band_rows], pad),
+    )
 
 
 def inverse_order(order):
@@ -421,6 +661,11 @@
     )
     fresh = own + (share * rainfall + force)
 
+    whole_lanes = 2 * MMAX // lat_bands == LANES and band_rows <= LANES
+    if lat_bands == 2 and whole_lanes and levels % lax.axis_size("col") == 0:
+        coeffs = spectral_step(fresh, wave_table)
+        return (fresh[None, None], coeffs[None, None])
+
     regrouped = lax.all_to_all(fresh, "col", split_axis=0, concat_axis=0, tiled=True)
     owner_count = MMAX // lat_bands
     wave_table, _ = lax.optimization_barrier((wave_table, rainfall))

time: 180 us -> 164 us (0.911)
  waiting for transfers between devices: 30.1 us -> 14.6 us
  Pallas kernels: 81.2 us -> 93.3 us
  starting transfers between devices: 23.1 us -> 11.8 us
  other arithmetic: 18.5 us -> 16.3 us
    all_to_all x2 -> x0, waiting for transfers between devices: 14.6 us -> none  [the longest x1 8.44 us: shards(): lax.all_to_all(fresh, 'col', split_axis=0, concat_axis=0, tiled=True)]
    pallas_call x3 -> x1, Pallas kernels: 32.2 us -> 44.3 us  [spectral_step(): pl.pallas_call(spectral_kernel, out_shape=jax.ShapeDtypeStruct((levels, s...]
    all_to_all x2 -> x0, starting transfers between devices: 9.4 us -> none  [the longest x1 5 us: shards(): lax.all_to_all(fresh, 'col', split_axis=0, concat_axis=0, tiled=True)]
    all_to_all x1, starting transfers between devices: 7.69 us -> 5.59 us  [shards(): lax.all_to_all(outgoing, ('sec', 'lat'), split_axis=0, concat_axis=0, til...]
  transfers between devices with their start and end apart: 5 -> 3, of which waited for: 4 -> 2; matrix products, arithmetic and copies ran while one was open for 16% -> 12% of each run, Pallas kernels for 11% -> 0%
where the time goes in v1:
time: 164 us; the launch traced here: 163 us
  Pallas kernels  93.3 us (57%)
  local copies, waits for them, and re-layouts  19.7 us (12%)
  other arithmetic  16.3 us (10%)
  waiting for transfers between devices  14.6 us (9%)
  starting transfers between devices  11.8 us (7%)
  matrix products  6.54 us (4%)
    pallas_call x1, Pallas kernels, spectral_step(): pl.pallas_call(spectral_kernel, out_shape=jax.ShapeDtypeStruct((levels, s...  44.3 us
    pallas_call x2, Pallas kernels, permute(): pl.pallas_call(permute_kernel, out_shape=jax.ShapeDtypeStruct(shape, jnp....  33.4 us
    pallas_call x1, Pallas kernels, cloud_model(): pl.pallas_call(cloud_kernel, grid=(bands * steps,), out_shape=jax.ShapeDt...  15.7 us
    all_to_all x1, waiting for transfers between devices, shards(): lax.all_to_all(outgoing, ('sec', 'lat'), split_axis=0, concat_axis=0, til...  8.26 us
    optimization_barrier x1, local copies, waits for them, and re-layouts, shards(): crm_moisture, outgoing = lax.optimization_barrier((crm_moisture, outgoing))  6.59 us
    dot_general x1, matrix products, inverse_order(): jnp.dot(left, low.astype(jnp.bfloat16), preferred_element_type=jnp.float32)  6.54 us
    all_to_all x1, waiting for transfers between devices, shards(): lax.all_to_all(homeward, ('sec', 'lat'), split_axis=0, concat_axis=0, til...  6.34 us
    reshape x2, local copies, waits for them, and re-layouts, shards(): rainfall = rainfall.reshape(levels, band_rows, lon_block)  5.82 us
  transfers between devices with their start and end apart: 3, of which 2 were waited for; matrix products, arithmetic and copies ran while one was open for 12% of the time, Pallas kernels for 0%

profile of v1, /device:TPU:0, one launch (start us, length us, event | category | flops | bytes accessed | tf_op | source)
XLA Modules:
  0.0 163.2 jit_solution(1398437427258344287)
XLA Ops:
  0.6 3.0 %bitcast_select_fusion = f32[28,96,96]{2,1,0:T(8,128)} fusion(f32[1,1,28,96,96]{4,3,2,1,0:T(8,128)} %param.5, f32[1,1,28,96,96]{4,3,2,1,0:T(8,128)} %param.6, pred[]{:T(512)S(6)} %eq.44), kind=kLoop, calls=%fused_computation.10 | loop fusion | flops 258048 | bytes 3096577 | tf_op jit(solution)/shard_map/jit(_where)/select_n | solution.py:639
  3.6 1.8 %collective-permute-start = (f32[28,96,96]{2,1,0:T(8,128)}, f32[28,96,96]{2,1,0:T(8,128)}, u32[]{:S(2)}, u32[]{:S(2)}) collective-permute-start(f32[28,96,96]{2,1,0:T(8,128)} %bitcast_select_fusion), channel_id=1, source_target_pairs={{16,24},{24,16},{17,25},{25,17},{18,26},{26,18},{19,27},{27,19},{2... | collective-permute-start | bytes 3096584 | tf_op jit(solution)/shard_map/ppermute | solution.py:639
  5.5 0.3 iota_compare_fusion.2
  5.9 0.1 pad_maximum_fusion
  6.0 2.0 %broadcast_select_fusion = bf16[2,72,9216]{2,1,0:T(8,128)(2,1)} fusion(pred[72,9216]{1,0:T(8,128)(4,1)S(1)} %iota_compare_fusion.2, bf16[2,9216]{1,0:T(2,128)(2,1)S(1)} %pad_maximum_fusion), kind=kLoop, calls=%fused_computation.4 | loop fusion | flops 1327104 | bytes 3354624 | tf_op jit(solution)/shard_map/jit(_where)/select_n | solution.py:622
  8.0 0.1 dynamic_slice.3
  8.1 0.1 mul.192
  8.4 0.2 copy-done.1
  8.6 2.8 %fusion.2 = f32[28,96,96]{2,1,0:T(8,128)} fusion(f32[28,96,96]{2,1,0:T(8,128)} %collective-permute-done, f32[1,1,28,96,96]{4,3,2,1,0:T(8,128)S(1)} %copy-done, f32[1,1,28,96,96]{4,3,2,1,0:T(8,128)S(1)} %copy-done.1, pred[]{:T(512)S(6)} %eq.44, pred[]{:T(512)S(6)} %eq.45), kind=kLoop, calls=%fused_computation.7 | loop fusion | flops 1290240 | bytes 4128770 | tf_op jit(solution)/shard_map/jit(_where)/select_n | solution.py:640
  11.4 3.2 %reshape.433.x_ref = f32[28,9216]{1,0:T(8,128)} reshape(f32[28,96,96]{2,1,0:T(8,128)} %fusion.2) | data formatting | bytes 2064384 | tf_op jit(solution)/shard_map/reshape | solution.py:643
  14.6 16.7 %permute.2 = f32[8,28,1152]{2,1,0:T(8,128)} custom-call(f32[28,9216]{1,0:T(8,128)} %reshape.433.x_ref, s32[1,9216]{1,0:T(1,128)} %bitcast.41), custom_call_target="tpu_custom_call" | custom-call | tf_op jit(solution)/shard_map/permute/pallas_call | solution.py:91
  31.3 5.6 %all-to-all-start = ((f32[8,28,1152]{2,1,0:T(8,128)}), f32[8,28,1152]{2,1,0:T(8,128)}, u32[]{:S(2)}, u32[]{:S(2)}) async-start(f32[8,28,1152]{2,1,0:T(8,128)} %permute.2), calls=%async_computation | async-start | bytes 2359296 | tf_op jit(solution)/shard_map/all_to_all | solution.py:652
  37.0 1.1 fusion.13
  38.1 6.6 %copy.9 = bf16[1,32,28,1,1,2304]{5,2,1,4,3,0:T(8,128)(2,1)} copy(bf16[1,32,28,1,1,2304]{5,1,4,3,2,0:T(8,128)(2,1)} %param.7) | data formatting | bytes 8257536 | tf_op jit(solution)/shard_map/optimization_barrier | solution.py:651
  44.7 8.3 %all-to-all-done.wind_ref.gap_ref.push_ref = f32[8,28,1152]{2,1,0:T(8,128)} async-done(((f32[8,28,1152]{2,1,0:T(8,128)}), f32[8,28,1152]{2,1,0:T(8,128)}, u32[]{:S(2)}, u32[]{:S(2)}) %all-to-all-start) | async-done | bytes 1032224 | tf_op jit(solution)/shard_map/all_to_all | solution.py:652
  53.0 15.7 %cloud.1 = f32[4,2,28,1152]{3,2,1,0:T(8,128)} custom-call(f32[8,28,1152]{2,1,0:T(8,128)} %all-to-all-done.wind_ref.gap_ref.push_ref, f32[8,28,1152]{2,1,0:T(8,128)} %all-to-all-done.wind_ref.gap_ref.push_ref, f32[8,28,1152]{2,1,0:T(8,128)} %all-to-all-done.wind_ref.gap_ref.push_ref, bf16[32,28,2304]{2,1,0:T(8,128)(2,1)} %bitcast.36), custom_call_target="tpu_custom_call" | custom-call | tf_op jit(solution)/shard_map/cloud/pallas_call | solution.py:160
  68.6 4.4 %all-to-all-start.1 = ((f32[8,28,1152]{2,1,0:T(8,128)}), f32[8,28,1152]{2,1,0:T(8,128)}, u32[]{:S(2)}, u32[]{:S(2)}) async-start(f32[8,28,1152]{2,1,0:T(8,128)} %bitcast.37), calls=%async_computation.1 | async-start | bytes 2359296 | tf_op jit(solution)/shard_map/all_to_all | solution.py:654
  73.1 0.6 pad.8.cosine_ref
  73.7 0.9 maximum_multiply_fusion
  74.6 6.5 %fusion.7 = s32[144,128]{1,0:T(8,128)S(1)} fusion(bf16[144,9216]{1,0:T(8,128)(2,1)} %bitcast.38, s32[9216]{0:T(1024)S(1)} %get-tuple-element.6), kind=kOutput, calls=%fused_computation.17 | convolution fusion | flops 340936704 | bytes 2764800 | tf_op jit(solution)/shard_map/dot_general | solution.py:623
  81.1 0.6 slice_add_fusion
  81.7 0.7 multiply_select_fusion
  82.5 6.3 %all-to-all-done.1.x_ref = f32[8,28,1152]{2,1,0:T(8,128)} async-done(((f32[8,28,1152]{2,1,0:T(8,128)}), f32[8,28,1152]{2,1,0:T(8,128)}, u32[]{:S(2)}, u32[]{:S(2)}) %all-to-all-start.1) | async-done | bytes 1032224 | tf_op jit(solution)/shard_map/all_to_all | solution.py:654
  88.8 16.7 %permute.3 = f32[28,9216]{1,0:T(8,128)} custom-call(f32[8,28,1152]{2,1,0:T(8,128)} %all-to-all-done.1.x_ref, s32[1,9216]{1,0:T(1,128)} %bitcast.43), custom_call_target="tpu_custom_call" | custom-call | tf_op jit(solution)/shard_map/permute/pallas_call | solution.py:91
  105.5 2.9 %reshape.435 = f32[1,1,28,96,96]{4,3,2,1,0:T(8,128)} reshape(f32[28,9216]{1,0:T(8,128)} %permute.3) | data formatting | bytes 2064384 | tf_op jit(solution)/shard_map/reshape | solution.py:658
  108.4 2.9 %reshape.436 = f32[28,96,96]{2,1,0:T(8,128)} reshape(f32[28,9216]{1,0:T(8,128)} %permute.3) | data formatting | bytes 2064384 | tf_op jit(solution)/shard_map/reshape | solution.py:658
  111.3 2.9 %add_add_fusion = f32[1,1,28,96,96]{4,3,2,1,0:T(8,128)} fusion(f32[1,1,28,96,96]{4,3,2,1,0:T(8,128)S(1)} %copy-done, f32[1,1,28,96,96]{4,3,2,1,0:T(8,128)S(1)} %copy-done.1, f32[1,1,28,96,96]{4,3,2,1,0:T(8,128)} %reshape.435, f32[]{:T(128)S(6)} %select_n.125, pred[]{:T(512)S(6)} %lt.24), kind=kLoop, calls=%fused_computation.16 | loop fusion | flops 1290240 | bytes 4128773 | tf_op jit(solution)/shard_map/add | solution.py:662
  114.3 1.5 bitcast_add_fusion.fresh_ref
  115.7 0.7 broadcast_in_dim.77.order_ref
  116.4 0.6 broadcast_in_dim.78.zero_ref
  117.0 44.3 %spectral.1 = f32[7,64,2,128]{3,2,1,0:T(2,128)} custom-call(f32[28,96,96]{2,1,0:T(8,128)} %bitcast_add_fusion.fresh_ref, f32[4,256,96]{2,1,0:T(8,128)} %bitcast.39, f32[64,128]{1,0:T(8,128)} %get-tuple-element.11.grow_ref, f32[64,128]{1,0:T(8,128)} %get-tuple-element.12.retreat_ref, s32[64,128]{1,0:T(8,128)} %broadcast_in_dim.77.order_ref, ...), custom_call_target="tpu_custom_call" | custom-call | tf_op jit(solution)/shard_map/spectral/pallas_call | solution.py:580
  161.3 1.8 %copy.11 = f32[1,1,7,64,2,128]{5,4,3,2,1,0:T(2,128)} copy(f32[1,1,7,64,2,128]{5,4,3,2,1,0:T(2,128)} %bitcast.40) | data formatting | bytes 917504
  (33 shorter events, 0.4 us)
Async XLA Ops:
  0.6 4.8 %copy-start.3 = (s32[1,1,9216]{2,1,0:T(1,128)S(1)}, s32[1,1,9216]{2,1,0:T(1,128)}, u32[]{:S(2)}) copy-start(s32[1,1,9216]{2,1,0:T(1,128)} %param.8) | copy-start | bytes 110596
  3.6 4.7 %collective-permute-start = (f32[28,96,96]{2,1,0:T(8,128)}, f32[28,96,96]{2,1,0:T(8,128)}, u32[]{:S(2)}, u32[]{:S(2)}) collective-permute-start(f32[28,96,96]{2,1,0:T(8,128)} %bitcast_select_fusion), channel_id=1, source_target_pairs={{16,24},{24,16},{17,25},{25,17},{18,26},{26,18},{19,27},{27,19},{2... | collective-permute-start | bytes 3096584 | tf_op jit(solution)/shard_map/ppermute | solution.py:639
  6.0 2.0 %copy-start.7 = (s32[128]{0:T(128)S(1)}, s32[128]{0:T(128)}, u32[]{:S(2)}) copy-start(s32[128]{0:T(128)} %param.9) | copy-start | bytes 1540
  6.0 2.4 %copy-start = (f32[1,1,28,96,96]{4,3,2,1,0:T(8,128)S(1)}, f32[1,1,28,96,96]{4,3,2,1,0:T(8,128)}, u32[]{:S(2)}) copy-start(f32[1,1,28,96,96]{4,3,2,1,0:T(8,128)} %param.5) | copy-start | bytes 3096580
  6.0 2.6 %copy-start.1 = (f32[1,1,28,96,96]{4,3,2,1,0:T(8,128)S(1)}, f32[1,1,28,96,96]{4,3,2,1,0:T(8,128)}, u32[]{:S(2)}) copy-start(f32[1,1,28,96,96]{4,3,2,1,0:T(8,128)} %param.6) | copy-start | bytes 3096580
  8.2 64.9 %copy-start.5 = (f32[192]{0:T(256)}, f32[192]{0:T(256)S(1)}, u32[]{:S(2)}) copy-start(f32[192]{0:T(256)S(1)} %fusion.23) | copy-start | bytes 2308
  8.3 64.8 %copy-start.6 = (f32[192]{0:T(256)}, f32[192]{0:T(256)S(1)}, u32[]{:S(2)}) copy-start(f32[192]{0:T(256)S(1)} %fusion.24) | copy-start | bytes 2308
  31.3 21.7 %all-to-all-start = ((f32[8,28,1152]{2,1,0:T(8,128)}), f32[8,28,1152]{2,1,0:T(8,128)}, u32[]{:S(2)}, u32[]{:S(2)}) async-start(f32[8,28,1152]{2,1,0:T(8,128)} %permute.2), calls=%async_computation | async-start | bytes 2359296 | tf_op jit(solution)/shard_map/all_to_all | solution.py:652
  68.6 20.2 %all-to-all-start.1 = ((f32[8,28,1152]{2,1,0:T(8,128)}), f32[8,28,1152]{2,1,0:T(8,128)}, u32[]{:S(2)}, u32[]{:S(2)}) async-start(f32[8,28,1152]{2,1,0:T(8,128)} %bitcast.37), calls=%async_computation.1 | async-start | bytes 2359296 | tf_op jit(solution)/shard_map/all_to_all | solution.py:654
  74.5 7.2 %copy-start.4 = (pred[128]{0:T(512)(128)(4,1)S(1)}, pred[128]{0:T(512)(128)(4,1)}, u32[]{:S(2)}) copy-start(pred[128]{0:T(512)(128)(4,1)} %constant.160.clone.1) | copy-start | bytes 388
  74.5 7.2 %slice-start = ((f32[192]{0:T(256)}), f32[128]{0:T(128)S(1)}, s32[]{:S(2)}) async-start(f32[192]{0:T(256)} %copy-done.5), calls=%async_computation.2 | async-start | bytes 1024 | tf_op jit(solution)/shard_map/slice
  74.6 7.2 %slice-start.1 = ((f32[192]{0:T(256)}), f32[128]{0:T(128)S(1)}, s32[]{:S(2)}) async-start(f32[192]{0:T(256)} %copy-done.6), calls=%async_computation.3 | async-start | bytes 1024 | tf_op jit(solution)/shard_map/slice
  111.3 2.9 %copy-start.2 = (f32[28,96,96]{2,1,0:T(8,128)S(1)}, f32[28,96,96]{2,1,0:T(8,128)}, u32[]{:S(2)}) copy-start(f32[28,96,96]{2,1,0:T(8,128)} %reshape.436) | copy-start | bytes 3096580

commit v2 on v1

--- a/solution.py
+++ b/solution.py
@@ -612,6 +612,454 @@
     )
 
 
+GROUP = ROWS
+DIGIT = 2 * LANES
+
+
+def physics_kernel(
+    own_ref,
+    force_ref,
+    anomaly_ref,
+    order_ref,
+    spread_ref,
+    fresh_ref,
+    own,
+    force,
+    mate,
+    anomaly,
+    parts,
+    held,
+    onehot,
+    stage,
+    arrived,
+    coef,
+    partial,
+    rain,
+    rain_in,
+    grid_sum,
+    shared,
+    load_sem,
+    mate_sem,
+    out_send,
+    out_recv,
+    back_send,
+    back_recv,
+    share_send,
+    share_recv,
+):
+    sec, lat = lax.axis_index("sec"), lax.axis_index("lat")
+    side, core = sec // 2, lax.rem(sec, 2)
+    bands = arrived.shape[1]
+    rows, span = arrived.shape[2], arrived.shape[3]
+    band_rows = fresh_ref.shape[1] and fresh_ref.shape[0] // anomaly.shape[0]
+    lon_block = own.shape[1]
+    levels, count, _ = anomaly.shape
+    groups = rows // GROUP
+    depth = levels // groups
+    tiles = order_ref.shape[1] // LANES
+    per = span // LANES
+    gathered = held.shape[1] // LANES
+    multiplied = tiles - gathered
+
+    def at(s, b):
+        return {"sec": s, "lat": b}
+
+    mate_sec = 2 * side + (1 - core)
+    across = 2 * (1 - side) + core
+    far = 2 * (1 - side) + (1 - core)
+
+    barrier = pltpu.get_barrier_semaphore()
+    for s in (mate_sec, across, far, sec):
+        for b in (1 - lat, lat):
+            if s is sec and b is lat:
+                continue
+            pl.semaphore_signal(barrier, inc=1, device_id=at(s, b), device_id_type=MESH_IDS)
+
+    used = levels * band_rows
+    loads = [
+        pltpu.make_async_copy(own_ref, own.at[pl.ds(0, used)], load_sem.at[0]),
+        pltpu.make_async_copy(force_ref, force.at[pl.ds(0, used)], load_sem.at[1]),
+        pltpu.make_async_copy(anomaly_ref, anomaly, load_sem.at[2]),
+    ]
+    for copy in loads:
+        copy.start()
+    pl.semaphore_wait(barrier, 4 * bands - 1)
+
+    def mate_copy(source):
+        return pltpu.make_async_remote_copy(
+            src_ref=source,
+            dst_ref=mate.at[pl.ds(0, used)],
+            send_sem=mate_sem.at[0],
+            recv_sem=mate_sem.at[1],
+            device_id=at(mate_sec, lat),
+            device_id_type=MESH_IDS,
+        )
+
+    @pl.when(sec == 2)
+    def _():
+        mate_copy(force_ref).start()
+
+    @pl.when(sec != 2)
+    def _():
+        mate_copy(own_ref).start()
+
+    beyond = own.shape[0] - used
+    for ref in (own, force, mate):
+        ref[used:] = jnp.zeros((beyond, lon_block), jnp.float32)
+
+    digit = lax.broadcasted_iota(jnp.int32, (DIGIT, LANES), 0)
+
+    def mark(t, carry):
+        lanes = pl.ds(pl.multiple_of(t * LANES, LANES), LANES)
+        low = order_ref[:, lanes] & (DIGIT - 1)
+        onehot[:, lanes] = jnp.where(digit == low, 1.0, 0.0).astype(jnp.bfloat16)
+        return carry
+
+    lax.fori_loop(0, tiles, mark, 0)
+    loads[0].wait()
+    loads[1].wait()
+    mate_copy(own_ref).wait()
+
+    quad = 4 * lon_block // LANES
+
+    def flatten(q, g):
+        found = []
+        for v in range(4):
+            at_rows = pl.ds(g * band_rows + q * 4 + v, GROUP, stride=groups * band_rows)
+            mine, push, other = own[at_rows, :], force[at_rows, :], mate[at_rows, :]
+            found.append(
+                jnp.where(
+                    sec == 3,
+                    (push - other) * (1.0 / NSUB),
+                    jnp.where(sec == 2, other - mine, mine),
+                )
+            )
+        out = []
+        for w in range(quad):
+            pieces = []
+            for v in range(4):
+                lo = max(w * LANES - v * lon_block, 0)
+                hi = min((w + 1) * LANES - v * lon_block, lon_block)
+                if lo < hi:
+                    pieces.append(found[v][:, lo:hi])
+            out.append(jnp.concatenate(pieces, axis=1))
+        return out
+
+    def split(q, carry):
+        for g in range(0, groups, 2):
+            for w, pair in enumerate(zip(flatten(q, g), flatten(q, g + 1))):
+                block = jnp.concatenate(pair, axis=0)
+                base = pl.multiple_of((q * quad + w) * rows + g * GROUP, 2 * GROUP)
+                coarse, fine = halve(block)
+                parts[pl.ds(base, 2 * GROUP), :LANES] = coarse
+                parts[pl.ds(base, 2 * GROUP), LANES:] = fine
+        return carry
+
+    def keep_whole(q, carry):
+        for g in range(groups):
+            for w, block in enumerate(flatten(q, g)):
+                lane0 = pl.multiple_of((q * quad + w) * LANES - multiplied * LANES, LANES)
+                held[g * GROUP : (g + 1) * GROUP, pl.ds(lane0, LANES)] = block
+        return carry
+
+    wanted = lax.broadcasted_iota(jnp.int32, (2 * LANES, 2 * LANES), 0) & (LANES - 1)
+
+    def permute_pair(dest, pair):
+        first = dest * bands * per + pair * 2
+        order = order_ref[:, pl.ds(pl.multiple_of(first * LANES, LANES), 2 * LANES)]
+        lane = order & (LANES - 1)
+        chosen = jnp.where(wanted == lane, 1.0, 0.0).astype(jnp.bfloat16)
+        moved = jnp.dot(parts[...], chosen, preferred_element_type=jnp.float32)
+        for h in range(2):
+            mine = slice(h * LANES, (h + 1) * LANES)
+            source = jnp.broadcast_to(order[:, mine] >> 7, (ROWS, LANES))
+            lanes = jnp.broadcast_to(lane[:, mine], (ROWS, LANES))
+            total = [jnp.zeros((ROWS, LANES), jnp.float32) for _ in range(groups)]
+            for s in range(gathered):
+                hit = source == multiplied + s
+                for r in range(groups):
+                    block = held[r * ROWS : (r + 1) * ROWS, s * LANES : (s + 1) * LANES]
+                    total[r] = jnp.where(hit, jnp.take_along_axis(block, lanes, axis=1), total[r])
+            for s in range(multiplied):
+                hit = source == s
+                for r in range(groups):
+                    begin = s * rows + r * ROWS
+                    total[r] = jnp.where(hit, moved[begin : begin + ROWS, mine], total[r])
+            tile = pair * 2 + h
+            to = pl.ds(pl.multiple_of(lax.rem(tile, per) * LANES, LANES), LANES)
+            for r in range(groups):
+                stage[dest, tile // per, r * ROWS : (r + 1) * ROWS, to] = total[r]
+
+    def out_copy(dest, b):
+        return pltpu.make_async_remote_copy(
+            src_ref=stage.at[dest, b],
+            dst_ref=arrived.at[sec, lat],
+            send_sem=out_send.at[dest, b],
+            recv_sem=out_recv.at[sec, lat],
+            device_id=at(dest, b),
+            device_id_type=MESH_IDS,
+        )
+
+    def out_local():
+        return pltpu.make_async_copy(
+            stage.at[sec, lat], arrived.at[sec, lat], out_recv.at[sec, lat]
+        )
+
+    @pl.when(sec != 1)
+    def _():
+        lax.fori_loop(0, multiplied // quad, split, 0)
+        lax.fori_loop(multiplied // quad, tiles // quad, keep_whole, 0)
+        for dest in (across, far, mate_sec, sec):
+
+            def pairs(p, carry, dest=dest):
+                permute_pair(dest, p)
+                return carry
+
+            lax.fori_loop(0, bands * per // 2, pairs, 0)
+            out_copy(dest, 1 - lat).start()
+            if dest is sec:
+                out_local().start()
+            else:
+                out_copy(dest, lat).start()
+
+    for field in (0, 2, 3):
+        for b in range(bands):
+            pltpu.make_async_copy(
+                arrived.at[field, b], arrived.at[field, b], out_recv.at[field, b]
+            ).wait()
+    loads[2].wait()
+
+    volumes = count // ROWS
+
+    def back_copy(dest, b):
+        return pltpu.make_async_remote_copy(
+            src_ref=rain.at[dest, b],
+            dst_ref=rain_in.at[sec * bands + lat],
+            send_sem=back_send.at[dest, b],
+            recv_sem=back_recv.at[sec * bands + lat],
+            device_id=at(dest, b),
+            device_id_type=MESH_IDS,
+        )
+
+    def back_local():
+        return pltpu.make_async_copy(
+            rain.at[sec, lat], rain_in.at[sec * bands + lat], back_recv.at[sec * bands + lat]
+        )
+
+    def cloud_group(dest):
+        at_rows = pl.ds(pl.multiple_of(dest * GROUP, GROUP), GROUP)
+        for b in range(bands):
+            for c in range(per):
+                lanes = slice(c * LANES, (c + 1) * LANES)
+                courant = COURANT_SCALE * jnp.tanh(arrived[0, b, at_rows, lanes])
+                mixing = 0.2 + 0.5 * jnp.abs(courant)
+                coef[0, b, c] = mixing - 0.5 * courant
+                coef[1, b, c] = mixing + 0.5 * courant
+                coef[2, b, c] = 1.0 - 2.0 * mixing
+                coef[3, b, c] = -arrived[2, b, at_rows, lanes]
+                coef[4, b, c] = -arrived[3, b, at_rows, lanes]
+
+        def level(r, carry):
+            for b in range(bands):
+                moist = jnp.dot(
+                    spread_ref[...],
+                    anomaly[r * groups + dest, :, b * span : (b + 1) * span],
+                    preferred_element_type=jnp.float32,
+                )
+                for c in range(per):
+                    lanes = slice(c * LANES, (c + 1) * LANES)
+                    ahead, back, keep, low, push = [
+                        coef[k, b, c, pl.ds(r, ROWS, stride=0), :] for k in range(5)
+                    ]
+                    start = [moist[v * ROWS : (v + 1) * ROWS, lanes] for v in range(volumes)]
+                    gap = start
+                    for substep in range(NSUB - 1):
+                        after = gap[1:] + [pltpu.roll(gap[0], ROWS - 1, axis=0)]
+                        before = [pltpu.roll(gap[-1], 1, axis=0)] + gap[:-1]
+                        gap = [
+                            (ahead * n + back * p) + (keep * x - jnp.maximum(x, low))
+                            for n, p, x in zip(after, before, gap)
+                        ]
+                        low = push
+                    total = None
+                    for x, y in zip(start, gap):
+                        term = x - jnp.minimum(y, push)
+                        total = term if total is None else total + term
+                    partial[b, pl.ds(pl.multiple_of(r * ROWS, ROWS), ROWS), lanes] = total
+            return carry
+
+        lax.fori_loop(0, depth, level, 0)
+        row = lax.broadcasted_iota(jnp.int32, (ROWS, LANES), 0)
+        for b in range(bands):
+            for c in range(per):
+                lanes = slice(c * LANES, (c + 1) * LANES)
+                found = -count * (coef[3, b, c] + (NSUB - 2) * coef[4, b, c])
+                for r in range(depth):
+                    sums = jnp.sum(partial[b, r * ROWS : (r + 1) * ROWS, lanes], axis=0, keepdims=True)
+                    found = jnp.where(row == r, found + sums, found)
+                rain[dest, b, :, lanes] = (CONDENSE / count) * found
+
+    for dest in (across, far, mate_sec, sec):
+        cloud_group(dest)
+        back_copy(dest, 1 - lat).start()
+        if dest is sec:
+            back_local().start()
+        else:
+            back_copy(dest, lat).start()
+
+    sources = rain_in.shape[0]
+    for k in range(sources):
+        pltpu.make_async_copy(rain_in.at[k], rain_in.at[k], back_recv.at[k]).wait()
+
+    digits = tiles * LANES // DIGIT
+    grid_sum[...] = jnp.zeros_like(grid_sum)
+    chunk = 3 * LANES
+
+    def scatter(k, carry):
+        halves = []
+        for w in range(chunk // LANES):
+            tile = k * (chunk // LANES) + w
+            at_lanes = pl.ds(pl.multiple_of(lax.rem(tile, per) * LANES, LANES), LANES)
+            coarse, fine = halve(rain_in[tile // per, :, at_lanes])
+            both = jnp.concatenate([coarse, fine], axis=0)
+            high = order_ref[:, pl.ds(pl.multiple_of(tile * LANES, LANES), LANES)] // DIGIT
+            high = jnp.broadcast_to(high.astype(jnp.bfloat16), both.shape)
+            halves.append(
+                jnp.concatenate(
+                    [jnp.where(high == d, both, jnp.bfloat16(0)) for d in range(digits)], axis=0
+                )
+            )
+        left = jnp.concatenate(halves, axis=1)
+        right = onehot[:, pl.ds(pl.multiple_of(k * chunk, LANES), chunk)]
+        grid_sum[...] += lanes_product(left, right)
+        return carry
+
+    lax.fori_loop(0, tiles * LANES // chunk, scatter, 0)
+
+    for d in range(digits):
+        found = grid_sum[d * 2 * ROWS : d * 2 * ROWS + ROWS] + grid_sum[
+            d * 2 * ROWS + ROWS : (d + 1) * 2 * ROWS
+        ]
+        for h in range(DIGIT // LANES):
+            tile = d * (DIGIT // LANES) + h
+            shared[sec, tile * ROWS : (tile + 1) * ROWS] = found[:, h * LANES : (h + 1) * LANES]
+
+    def share_copy(kind, group, dest):
+        return pltpu.make_async_remote_copy(
+            src_ref=shared.at[group],
+            dst_ref=shared.at[group],
+            send_sem=share_send.at[kind],
+            recv_sem=share_recv.at[kind],
+            device_id=at(dest, lat),
+            device_id_type=MESH_IDS,
+        )
+
+    share_copy(0, sec, across).start()
+    share_copy(1, sec, mate_sec).start()
+
+    def update(group):
+        def one(r, carry):
+            base = (r * groups + group) * band_rows
+            for q in range(0, band_rows // 4, ROWS):
+                pieces = [
+                    shared[group, pl.ds((q * quad + w) * ROWS + r, ROWS, stride=quad * ROWS), :]
+                    for w in range(quad)
+                ]
+                for v in range(4):
+                    cut = []
+                    for w in range(quad):
+                        lo = max(v * lon_block - w * LANES, 0)
+                        hi = min((v + 1) * lon_block - w * LANES, LANES)
+                        if lo < hi:
+                            cut.append(pieces[w][:, lo:hi])
+                    found = cut[0] if len(cut) == 1 else jnp.concatenate(cut, axis=1)
+                    at_rows = pl.ds(base + q * 4 + v, ROWS, stride=4)
+                    mine = own[at_rows, :]
+                    share = jnp.where(
+                        sec < 2,
+                        mine * (-1.0 / NSUB),
+                        jnp.where(sec == 2, jnp.float32(1), jnp.float32(-1)),
+                    )
+                    fresh_ref[at_rows, :] = mine + (share * found + force[at_rows, :])
+            return carry
+
+        lax.fori_loop(0, depth, one, 0)
+
+    update(sec)
+    share_copy(1, mate_sec, mate_sec).wait_recv()
+    update(mate_sec)
+    share_copy(0, across, across).wait_recv()
+    share_copy(2, across, mate_sec).start()
+    update(across)
+    share_copy(2, far, mate_sec).wait_recv()
+    update(far)
+
+    share_copy(0, sec, across).wait_send()
+    share_copy(1, sec, mate_sec).wait_send()
+    share_copy(2, across, mate_sec).wait_send()
+    for dest in (across, far, mate_sec, sec):
+        for b in (1 - lat, lat):
+            if dest is sec and b is lat:
+                continue
+            back_copy(dest, b).wait_send()
+
+            @pl.when(sec != 1)
+            def _(dest=dest, b=b):
+                out_copy(dest, b).wait_send()
+
+
+def physics_step(own, force, anomaly, order):
+    levels, band_rows, lon_block = own.shape
+    _, count, width = anomaly.shape
+    sections, bands = lax.axis_size("sec"), lax.axis_size("lat")
+    tiles = order.shape[0] // LANES
+    span = width // bands
+    rows = GROUP * sections
+    gathered = tiles * 3 // 8
+    volumes = count // ROWS
+    index = jnp.arange(count, dtype=jnp.int32)
+    spread = (index % ROWS * volumes + index // ROWS)[:, None] == index[None, :]
+    flat = (levels * band_rows, lon_block)
+    padded = (rows * band_rows, lon_block)
+    anywhere = pl.BlockSpec(memory_space=pl.ANY)
+    vmem = pl.BlockSpec(memory_space=pltpu.VMEM)
+    f32, bf16 = jnp.float32, jnp.bfloat16
+    fresh = pl.pallas_call(
+        physics_kernel,
+        out_shape=jax.ShapeDtypeStruct(flat, f32),
+        in_specs=[anywhere] * 3 + [vmem] * 2,
+        out_specs=vmem,
+        scratch_shapes=[
+            pltpu.VMEM(padded, f32),
+            pltpu.VMEM(padded, f32),
+            pltpu.VMEM(padded, f32),
+            pltpu.VMEM(anomaly.shape, bf16),
+            pltpu.VMEM(((tiles - gathered) * rows, 2 * LANES), bf16),
+            pltpu.VMEM((rows, gathered * LANES), f32),
+            pltpu.VMEM((DIGIT, tiles * LANES), bf16),
+            pltpu.VMEM((sections, bands, rows, span), f32),
+            pltpu.VMEM((sections, bands, rows, span), f32),
+            pltpu.VMEM((5, bands, span // LANES, GROUP, LANES), f32),
+            pltpu.VMEM((bands, levels // sections * ROWS, span), f32),
+            pltpu.VMEM((sections, bands, GROUP, span), f32),
+            pltpu.VMEM((sections * bands, GROUP, span), f32),
+            pltpu.VMEM((tiles * LANES // DIGIT * 2 * GROUP, DIGIT), f32),
+            pltpu.VMEM((sections, tiles * GROUP, LANES), f32),
+            pltpu.SemaphoreType.DMA((3,)),
+            pltpu.SemaphoreType.DMA((2,)),
+            pltpu.SemaphoreType.DMA((sections, bands)),
+            pltpu.SemaphoreType.DMA((sections, bands)),
+            pltpu.SemaphoreType.DMA((sections, bands)),
+            pltpu.SemaphoreType.DMA((sections * bands,)),
+            pltpu.SemaphoreType.DMA((3,)),
+            pltpu.SemaphoreType.DMA((3,)),
+        ],
+        compiler_params=pltpu.CompilerParams(collective_id=0, has_side_effects=True),
+        name="physics",
+    )(own.reshape(flat), force.reshape(flat), anomaly, order[None, :], spread.astype(bf16))
+    return fresh.reshape(own.shape)
+
+
 def inverse_order(order):
     cols = order.shape[0]
     tiles = cols // LANES
@@ -635,6 +1083,15 @@
     field = lax.axis_index("sec")
     slot_list = cloud_order[0, 0]
     own, force = state[0, 0], forcing[0, 0]
+
+    aligned = per_target % LANES == 0 and (block_cols // LANES) % 24 == 0
+    grouped = sections == 4 and levels % sections == 0 and levels // sections <= GROUP
+    squared = band_rows % 32 == 0 and 4 * lon_block % LANES == 0 and crm_moisture.shape[1] % ROWS == 0
+    if lat_bands == 2 and aligned and grouped and squared and NSUB > 2:
+        moisture = crm_moisture[0, :, :, 0, 0, :].transpose(1, 0, 2)
+        fresh = physics_step(own, force, moisture, slot_list)
+        coeffs = spectral_step(fresh, wave_table)
+        return (fresh[None, None], coeffs[None, None])
 
     mate = lax.ppermute(jnp.where(field == 2, force, own), "sec", [(2, 3), (3, 2)])
     part = jnp.where(

time: 164 us -> 118 us (0.72)
  local copies, waits for them, and re-layouts: 19.7 us -> 4.03 us
  Pallas kernels: 93.3 us -> 108 us
  waiting for transfers between devices: 14.6 us -> 0 us
  starting transfers between devices: 11.8 us -> 0 us
  other arithmetic: 16.3 us -> 5.03 us
  matrix products: 6.54 us -> 0 us
    pallas_call x3 -> x1, Pallas kernels: 49.1 us -> 63.9 us  [physics_step(): pl.pallas_call(physics_kernel, out_shape=jax.ShapeDtypeStruct(flat, f32),...]
    all_to_all x2 -> x0, waiting for transfers between devices: 14.6 us -> none  [the longest x1 8.26 us: shards(): lax.all_to_all(outgoing, ('sec', 'lat'), split_axis=0, concat_axis=0, til...]
    all_to_all x2 -> x0, starting transfers between devices: 10 us -> none  [the longest x1 5.59 us: shards(): lax.all_to_all(outgoing, ('sec', 'lat'), split_axis=0, concat_axis=0, til...]
    reshape x3 -> x0, local copies, waits for them, and re-layouts: 9.01 us -> none  [the longest x2 5.82 us: shards(): rainfall = rainfall.reshape(levels, band_rows, lon_block)]
    select_n x4 -> x0, other arithmetic: 7.8 us -> none  [the longest x1 3 us: shards(): jnp.where(field == 2, force, own)]
    optimization_barrier x1 -> x0, local copies, waits for them, and re-layouts: 6.59 us -> none  [shards(): crm_moisture, outgoing = lax.optimization_barrier((crm_moisture, outgoing))]
    dot_general x1 -> x0, matrix products: 6.54 us -> none  [inverse_order(): jnp.dot(left, low.astype(jnp.bfloat16), preferred_element_type=jnp.float32)]
    add x3 -> x1, other arithmetic: 5.03 us -> 0.01 us  [physics_step(): spread = (index % ROWS * volumes + index // ROWS)[:, None] == index[None, :]]
  transfers between devices with their start and end apart: 3 -> 0, of which waited for: 2 -> 0; matrix products, arithmetic and copies ran while one was open for 12% -> 0% of each run, Pallas kernels for 0% -> 0%
where the time goes in v2:
time: 118 us
  Pallas kernels  108 us (92%)
  other arithmetic  5.03 us (4%)
  local copies, waits for them, and re-layouts  4.03 us (3%)
    pallas_call x1, Pallas kernels, physics_step(): pl.pallas_call(physics_kernel, out_shape=jax.ShapeDtypeStruct(flat, f32),...  63.9 us
    pallas_call x1, Pallas kernels, spectral_step(): pl.pallas_call(spectral_kernel, out_shape=jax.ShapeDtypeStruct((levels, s...  44.4 us

profile of v2, /device:TPU:0, one launch (start us, length us, event | category | flops | bytes accessed | tf_op | source)
XLA Modules:
  0.0 118.1 jit_solution(11284887449714747404)
XLA Ops:
  0.7 0.7 pad_add_fusion
  1.4 0.1 dynamic_slice.3
  1.5 0.1 mul.174
  1.7 0.5 pad.8.cosine_ref
  2.3 0.1 subtract_multiply_fusion
  2.4 0.7 fusion.9.spread_ref
  3.0 0.7 broadcast_in_dim.42.order_ref
  3.7 1.4 %multiply_select_fusion = (f32[64,128]{1,0:T(8,128)}, f32[64,128]{1,0:T(8,128)}, f32[64,128]{1,0:T(8,128)}) fusion(f32[128]{0:T(128)S(1)} %slice.15, f32[64]{0:T(128)S(1)} %get-tuple-element.7, f32[128]{0:T(128)S(1)} %slice.14, f32[64]{0:T(128)S(1)} %get-tuple-element.10, pred[128]{0:T(512)(128)(4,1)} %constant.128.clone.1, f32[64]{0:T(128)S(1)} %get-tuple-element.8, ...), kind=kLoop, calls=%fused_computation.14 | loop fusion | flops 106496 | bytes 102784 | tf_op jit(solution)/shard_map/jit(_pad)/pad | solution.py:611
  5.1 1.1 fusion.5
  6.2 0.9 maximum_multiply_fusion
  7.1 63.9 %physics.1 = f32[2688,96]{1,0:T(8,128)} custom-call(f32[2688,96]{1,0:T(8,128)} %bitcast.19, f32[2688,96]{1,0:T(8,128)} %bitcast.20, bf16[28,32,2304]{2,1,0:T(8,128)(2,1)} %bitcast.16, s32[1,9216]{1,0:T(1,128)} %bitcast.21, bf16[32,32]{1,0:T(8,128)(2,1)} %fusion.9.spread_ref), custom_call_target="tpu_custom_call" | custom-call | tf_op jit(solution)/shard_map/physics/pallas_call | solution.py:1027
  71.0 0.0 copy-start
  71.0 0.6 broadcast_in_dim.43.zero_ref
  71.6 44.4 %spectral.1 = f32[7,64,2,128]{3,2,1,0:T(2,128)} custom-call(f32[28,96,96]{2,1,0:T(8,128)} %bitcast.14, f32[4,256,96]{2,1,0:T(8,128)} %bitcast.17, f32[64,128]{1,0:T(8,128)} %get-tuple-element.5.grow_ref, f32[64,128]{1,0:T(8,128)} %get-tuple-element.6.retreat_ref, s32[64,128]{1,0:T(8,128)} %broadcast_in_dim.42.order_ref, ...), custom_call_target="tpu_custom_call" | custom-call | tf_op jit(solution)/shard_map/spectral/pallas_call | solution.py:580
  116.0 0.0 copy-done
  116.0 0.0 copy-start.1
  116.0 1.1 copy.9
  117.1 0.2 copy-done.1
  117.3 0.8 copy.10
  (12 shorter events, 0.2 us)
Async XLA Ops:
  71.0 45.0 %copy-start = (f32[2688,96]{1,0:T(8,128)S(1)}, f32[2688,96]{1,0:T(8,128)}, u32[]{:S(2)}) copy-start(f32[2688,96]{1,0:T(8,128)} %physics.1) | copy-start | bytes 3096580
  116.0 1.3 %copy-start.1 = (f32[7,64,2,128]{3,2,1,0:T(2,128)S(1)}, f32[7,64,2,128]{3,2,1,0:T(2,128)}, u32[]{:S(2)}) copy-start(f32[7,64,2,128]{3,2,1,0:T(2,128)} %spectral.1) | copy-start | bytes 1376260
